TPU v7x, 256 devices: a whole 4x4x8 slice. The times are simulated.
256 devices in a mesh: expert: 16 (over y, x), tensor: 16 (over z, core).
Axes of the slice: x: 4, y: 4, z: 8, core: 2. Of those that a mesh axis runs over, the one named last changes fastest.
Arguments:
- queries: bfloat16 [4096, 8192], P('expert', 'tensor'), may hold values from -8 to 8
- keys_values: bfloat16 [16, 4, 1280, 256], P('expert'), may hold values from -6 to 6
- prefix_len: int32 [16], P('expert'), may hold values from 128 to 1024, as said below
- out_proj: bfloat16 [8192, 4096], P('tensor', 'expert'), may hold values from -0.0625 to 0.0625
- residual: bfloat16 [4096, 4096], P(('expert', 'tensor')), may hold values from -1.796875 to 1.796875
- norm_gain: float32 [4096], replicated, may hold values from 0.1 to 1.9
- expert_ids: int32 [4096, 8], P('expert'), may hold values from 0 to 63, all different within a row; in each aligned block of 16 rows (0 to 15, 16 to 31, ...) at most 3 rows name the same one
- route_weights: bfloat16 [4096, 8], P('expert'), may hold values from 0.19921875 to 1
- w_gate: bfloat16 [256, 4096, 384], P(('expert', 'tensor')), may hold values from -0.09375 to 0.09375
- w_up: bfloat16 [256, 4096, 384], P(('expert', 'tensor')), may hold values from -0.09375 to 0.09375
- w_down: bfloat16 [256, 384, 4096], P(('expert', 'tensor')), may hold values from -0.15625 to 0.15625
Outputs:
- layer_out: bfloat16 [4096, 4096], P(('expert', 'tensor'))
Inputs may be any that keep to these rules, and one draw needn't show every extreme that they name: `expert_ids`: in the rows of one device (aligned blocks of 16 rows) no expert is named by more than 3 rows, a bound that some block reaches; a row names 8 different experts. `prefix_len`: some sequence has all 1024 slots live.
All inputs are finite; a program needn't handle non-finite values.
Results may differ from a plain program's by a relative error of at most 0.035.
Values may be sent and summed in bfloat16 or wider, within the bound.
No kernel may reach another device: no remote copies, remote signals or barrier semaphores. Data moves between devices by JAX's collectives and lax.ppermute only.
A program may use at most 128 MiB of HBM per device.

v0:
```python
import math
import jax
import jax.numpy as jnp
from jax import lax
from jax.sharding import PartitionSpec as P

HEADS = 64
KVH = 4
HD = 128
TOPK = 8
HSPLIT = 4
TOK_DEV = 16
PREFIX = 1024


def norm_rows(hidden_state, norm_gain):
    values = hidden_state.astype(jnp.float32)
    factor = lax.rsqrt(jnp.mean(values * values, axis=-1, keepdims=True) + 1e-06)
    return (values * factor * norm_gain[None, :]).astype(jnp.bfloat16)


def route_tables(expert_ids, route_weights, experts, most_rows):
    total_rows = expert_ids.shape[0]
    named_mask = expert_ids[:, :, None] == jnp.arange(experts, dtype=jnp.int32)[None, None, :]
    hit_table = jnp.sum(named_mask.astype(jnp.int32), axis=1)
    weight_table = jnp.sum(
        jnp.where(named_mask, route_weights[:, :, None].astype(jnp.float32), 0.0), axis=1
    )
    grouped = hit_table.reshape(total_rows // TOK_DEV, TOK_DEV, experts)
    rank_table = (jnp.cumsum(grouped, axis=1) - grouped).reshape(total_rows, experts)
    share_index = (jnp.arange(total_rows, dtype=jnp.int32) // TOK_DEV)[:, None]
    position_table = share_index * most_rows + rank_table
    return (hit_table, weight_table, rank_table, position_table)


def pick_slot(table, expert_count, slot_count, slot_index):
    shaped = table.reshape(table.shape[0], expert_count, slot_count)
    return lax.dynamic_index_in_dim(shaped, slot_index, 2, keepdims=False)


def shards(
    queries,
    keys_values,
    prefix_len,
    out_proj,
    residual,
    norm_gain,
    expert_ids,
    route_weights,
    w_gate,
    w_up,
    w_down,
):
    tensor_count = lax.axis_size("tensor")
    expert_count = lax.axis_size("expert")
    tensor_index = lax.axis_index("tensor")
    step_rows = queries.shape[0]
    per_device = queries.shape[1] // HD
    group_size = HEADS // KVH
    kv_index = tensor_index * per_device // group_size
    cached = lax.dynamic_index_in_dim(keys_values[0], kv_index, 0, keepdims=False)
    key_rows = cached[:, :HD]
    value_rows = cached[:, HD:]
    context = cached.shape[0]
    query_rows = queries.reshape(step_rows, per_device, HD)
    scores = jnp.einsum(
        "nhd,cd->hnc", query_rows, key_rows, preferred_element_type=jnp.float32
    ) / math.sqrt(HD)
    columns = jnp.arange(context, dtype=jnp.int32)[None, :]
    positions = jnp.arange(step_rows, dtype=jnp.int32)[:, None]
    visible = ((columns < prefix_len[0]) | (columns >= PREFIX) & (columns - PREFIX <= positions))[
        None
    ]
    highest = jnp.max(jnp.where(visible, scores, -1e30), axis=-1, keepdims=True)
    weights = jnp.exp(jnp.where(visible, scores - highest, -1e30))
    summed = jnp.sum(weights, axis=-1)
    blended = jnp.einsum(
        "hnc,cd->nhd", weights.astype(jnp.bfloat16), value_rows, preferred_element_type=jnp.float32
    )
    attended = (
        (blended / jnp.transpose(summed)[:, :, None])
        .astype(jnp.bfloat16)
        .reshape(step_rows, per_device * HD)
    )
    head_part = jnp.dot(
        attended,
        lax.all_gather(out_proj, "expert", axis=1, tiled=True),
        preferred_element_type=jnp.float32,
    )
    slot_count = tensor_count // HSPLIT
    experts = expert_count * slot_count
    most_rows = min(TOK_DEV, max(2, TOK_DEV * TOPK // experts + 1))
    capacity = tensor_count * most_rows
    slot_index = tensor_index // HSPLIT
    start_row = tensor_index * TOK_DEV
    hit_table, weight_table, rank_table, position_table = route_tables(
        expert_ids, route_weights, experts, most_rows
    )
    hit_slot = pick_slot(hit_table, expert_count, slot_count, slot_index)
    weight_slot = pick_slot(weight_table, expert_count, slot_count, slot_index)
    position_slot = pick_slot(position_table, expert_count, slot_count, slot_index)
    slot_match = (hit_slot[:, :, None] == 1) & (
        position_slot[:, :, None] == jnp.arange(capacity, dtype=jnp.int32)[None, None, :]
    )
    head_sum = lax.psum(head_part.astype(jnp.bfloat16), "tensor").astype(jnp.float32)
    residual_full = lax.all_gather(residual, "tensor", axis=0, tiled=True)
    state_full = (residual_full.astype(jnp.float32) + head_sum).astype(jnp.bfloat16)
    hidden_state = lax.dynamic_slice_in_dim(state_full, start_row, TOK_DEV, 0)
    normed_full = norm_rows(state_full, norm_gain)
    source_rows = jnp.sum(
        jnp.where(slot_match, jnp.arange(step_rows, dtype=jnp.int32)[:, None, None], 0), axis=0
    )
    filled = jnp.any(slot_match, axis=0)
    outgoing = jnp.where(
        filled[:, :, None], jnp.take(normed_full, source_rows, axis=0), jnp.zeros((), jnp.bfloat16)
    )
    arrived_rows = lax.all_to_all(outgoing, "expert", split_axis=0, concat_axis=0, tiled=True)
    flat_rows = arrived_rows.reshape(-1, arrived_rows.shape[-1])
    gate_val = jnp.dot(flat_rows, w_gate[0], preferred_element_type=jnp.float32)
    up_val = jnp.dot(flat_rows, w_up[0], preferred_element_type=jnp.float32)
    inner = (jax.nn.silu(gate_val) * up_val).astype(jnp.bfloat16)
    result = jnp.dot(inner, w_down[0], preferred_element_type=jnp.float32).astype(jnp.bfloat16)
    computed = result.reshape(arrived_rows.shape)
    returned = lax.all_to_all(computed, "expert", split_axis=0, concat_axis=0, tiled=True)
    combine_weights = jnp.where(slot_match, weight_slot[:, :, None], 0.0).astype(jnp.bfloat16)
    expert_part = jnp.einsum(
        "njc,jcd->nd", combine_weights, returned, preferred_element_type=jnp.float32
    )
    expert_share = lax.psum_scatter(
        expert_part.astype(jnp.bfloat16), "tensor", scatter_dimension=0, tiled=True
    ).astype(jnp.float32)
    return (hidden_state.astype(jnp.float32) + expert_share).astype(jnp.bfloat16)


def solution(mesh):
    return jax.shard_map(
        shards,
        mesh=mesh,
        in_specs=(
            P("expert", "tensor"),
            P("expert", None, None, None),
            P("expert"),
            P("tensor", "expert"),
            P(("expert", "tensor"), None),
            P(),
            P("expert", None),
            P("expert", None),
            P(("expert", "tensor"), None, None),
            P(("expert", "tensor"), None, None),
            P(("expert", "tensor"), None, None),
        ),
        out_specs=P(("expert", "tensor"), None),
        check_vma=False,
    )
```

profile of v0, /device:TPU:2, one launch (start us, length us, event | category | flops | bytes accessed | tf_op | source)
XLA Modules:
  0.0 520.2 jit_solution(15658658182001831944)
XLA Ops:
  6.5 0.0 copy-start
  6.5 0.0 all-gather.5.cloned.1.call-start
  6.5 0.7 all-gather.5.cloned.1.call-update
  7.3 0.0 all-gather.3.cloned.1.call-start
  7.3 0.7 all-gather.3.cloned.1.call-update
  8.0 0.0 all-reduce.2.cloned.1.call-start
  8.1 0.8 convert_reduce_fusion
  8.9 0.1 copy.36
  9.7 1.1 copy.38
  10.7 1.9 reduce_window_sum.14
  12.7 2.0 dynamic-slice_bitcast_fusion
  14.7 1.0 fusion.26
  15.7 5.1 fusion.62
  20.8 2.4 fusion.33
  23.2 51.8 %all-gather.5.cloned.1.call-done = bf16[512,4096]{1,0:T(8,128)(2,1)} async-done(((bf16[512,256]{1,0:T(8,128)(2,1)}), bf16[512,4096]{1,0:T(8,128)(2,1)}) %all-gather.5.cloned.1.call-update) | async-done | bytes 4194320 | tf_op jit(solution)/shard_map/all_gather | solution.py:87
  75.0 4.8 convolution_convert_fusion.1
  79.8 0.0 all-reduce.2.cloned.1.call-update
  79.8 0.9 fusion.57
  80.8 0.4 select_reduce_fusion
  81.2 0.1 reshape.155
  81.2 0.4 fusion.37
  81.6 34.7 %all-gather.3.cloned.1.call-done = bf16[256,4096]{1,0:T(8,128)(2,1)} async-done(((bf16[16,4096]{1,0:T(8,128)(2,1)}), bf16[256,4096]{1,0:T(8,128)(2,1)}) %all-gather.3.cloned.1.call-update) | async-done | bytes 2097168 | tf_op jit(solution)/shard_map/all_gather | solution.py:106
  116.4 115.7 %all-reduce.2.cloned.1.call-done = bf16[256,4096]{1,0:T(8,128)(2,1)} async-done(((bf16[256,4096]{1,0:T(8,128)(2,1)}), bf16[256,4096]{1,0:T(8,128)(2,1)}) %all-reduce.2.cloned.1.call-update) | async-done | bytes 2097168 | tf_op jit(solution)/shard_map/psum | solution.py:105
  232.1 3.2 fusion.6
  235.2 0.0 copy-start.1
  235.3 1.3 copy-done.1
  236.6 0.0 copy-done.3
  236.6 2.0 fusion.8
  238.6 13.8 %gather_fusion = bf16[768,4096]{1,0:T(8,128)(2,1)} fusion(bf16[256,4096]{1,0:T(8,128)(2,1)} %fusion.8, s32[1024]{0:T(1024)S(1)} %pad_clamp_fusion), kind=kCustom, calls=%fused_computation | custom fusion | bytes 12585984 | tf_op jit(solution)/shard_map/jit(_take)/gather | solution.py:115
  252.4 3.9 select_select_fusion
  256.3 0.0 copy-start.5
  256.3 79.0 %all_to_all.10 = bf16[16,48,4096]{2,1,0:T(8,128)(2,1)S(1)} all-to-all(bf16[16,48,4096]{2,1,0:T(8,128)(2,1)S(1)} %select_select_fusion), channel_id=1, replica_groups=mesh['expert'=16,'tensor'=16] {'expert'}, dimensions={0} | all-to-all | bytes 12582912 | tf_op jit(solution)/shard_map/all_to_all | solution.py:117
  335.3 0.0 copy-done.5
  335.3 3.4 fusion.12
  338.7 0.0 copy-done.6
  338.7 3.5 fusion.22
  342.2 0.0 copy-done
  342.2 5.4 %convolution_convert_fusion = bf16[768,4096]{1,0:T(8,128)(2,1)} fusion(bf16[768,384]{1,0:T(8,128)(2,1)S(1)} %fusion.22, bf16[1,384,4096]{2,1,0:T(8,128)(2,1)S(1)} %copy-done), kind=kOutput, calls=%fused_computation.2 | convolution fusion | flops 2419064832 | bytes 10027008 | tf_op jit(solution)/shard_map/dot_general | solution.py:122
  347.6 6.0 %all-to-all-start.1 = ((bf16[16,48,4096]{2,1,0:T(8,128)(2,1)}), bf16[16,48,4096]{2,1,0:T(8,128)(2,1)}, u32[]{:S(2)}, u32[]{:S(2)}) async-start(bf16[16,48,4096]{2,1,0:T(8,128)(2,1)} %bitcast.108), calls=%async_computation.1 | async-start | bytes 12582912 | tf_op jit(solution)/shard_map/all_to_all | solution.py:124
  353.6 0.0 reduce-scatter.2.cloned.1.call-start
  353.6 0.0 copy-done.4
  353.7 0.0 copy-done.2
  353.7 0.1 select_reduce_fusion.1
  353.8 87.2 %all-to-all-done.1 = bf16[16,48,4096]{2,1,0:T(8,128)(2,1)} async-done(((bf16[16,48,4096]{2,1,0:T(8,128)(2,1)}), bf16[16,48,4096]{2,1,0:T(8,128)(2,1)}, u32[]{:S(2)}, u32[]{:S(2)}) %all-to-all-start.1) | async-done | bytes 6291488 | tf_op jit(solution)/shard_map/all_to_all | solution.py:124
  441.0 6.0 %fusion.3 = bf16[256,4096]{1,0:T(8,128)(2,1)} fusion(bf16[16,48,4096]{2,1,0:T(8,128)(2,1)} %all-to-all-done.1, bf16[256,16]{0,1:T(8,128)(2,1)S(1)} %bitcast.119, s32[256,16]{0,1:T(8,128)S(1)} %bitcast.113, pred[256,16]{0,1:T(8,128)(4,1)S(1)} %bitcast.118), kind=kOutput, calls=%fused_computation.11 | convolution fusion | flops 1612251136 | bytes 8417280 | tf_op jit(solution)/shard_map/njc,jcd->nd/dot_general | solution.py:126
  447.0 0.0 reduce-scatter.2.cloned.1.call-update
  447.0 65.0 %reduce-scatter.2.cloned.1.call-done = bf16[16,4096]{1,0:T(8,128)(2,1)} async-done(((bf16[256,4096]{1,0:T(8,128)(2,1)}), bf16[16,4096]{1,0:T(8,128)(2,1)}) %reduce-scatter.2.cloned.1.call-update) | async-done | bytes 131088 | tf_op jit(solution)/shard_map/reduce_scatter | solution.py:129
  512.0 1.7 add_convert_fusion.1
  (20 shorter events, 0.2 us)
Async XLA Ops:
  6.5 335.7 %copy-start = (bf16[1,384,4096]{2,1,0:T(8,128)(2,1)S(1)}, bf16[1,384,4096]{2,1,0:T(8,128)(2,1)}, u32[]{:S(2)}) copy-start(bf16[1,384,4096]{2,1,0:T(8,128)(2,1)} %param.21) | copy-start | bytes 9437188
  6.5 68.5 %all-gather.5.cloned.1.call-start = ((), (), s32[]{:S(2)}) async-start(), calls=%async_computation.4 | async-start | bytes 4456448 | tf_op jit(solution)/shard_map/all_gather | solution.py:87
  7.3 109.1 %all-gather.3.cloned.1.call-start = ((), (), s32[]{:S(2)}) async-start(), calls=%async_computation.3 | async-start | bytes 2228224 | tf_op jit(solution)/shard_map/all_gather | solution.py:106
  8.0 224.1 %all-reduce.2.cloned.1.call-start = ((), (), s32[]{:S(2)}) async-start(), calls=%async_computation.5 | async-start | bytes 4194304 | tf_op jit(solution)/shard_map/psum | solution.py:105
  79.8 156.8 %copy-start.3 = (f32[4096]{0:T(1024)S(1)}, f32[4096]{0:T(1024)}, u32[]{:S(2)}) copy-start(f32[4096]{0:T(1024)} %param.16) | copy-start | bytes 49156
  235.2 1.4 copy-start.1
  256.3 79.0 %copy-start.5 = (bf16[1,4096,384]{2,1,0:T(8,128)(2,1)S(1)}, bf16[1,4096,384]{2,1,0:T(8,128)(2,1)}, u32[]{:S(2)}) copy-start(bf16[1,4096,384]{2,1,0:T(8,128)(2,1)} %param.19) | copy-start | bytes 9437188
  335.3 3.4 copy-start.6
  347.6 6.0 %copy-start.4 = (bf16[256,8]{0,1:T(8,128)(2,1)S(1)}, bf16[256,8]{0,1:T(8,128)(2,1)}, u32[]{:S(2)}) copy-start(bf16[256,8]{0,1:T(8,128)(2,1)} %param.18) | copy-start | bytes 12292
  347.6 6.0 %copy-start.2 = (s32[256,8]{0,1:T(8,128)S(1)}, s32[256,8]{0,1:T(8,128)}, u32[]{:S(2)}) copy-start(s32[256,8]{0,1:T(8,128)} %param.17) | copy-start | bytes 24580
  347.6 93.4 %all-to-all-start.1 = ((bf16[16,48,4096]{2,1,0:T(8,128)(2,1)}), bf16[16,48,4096]{2,1,0:T(8,128)(2,1)}, u32[]{:S(2)}, u32[]{:S(2)}) async-start(bf16[16,48,4096]{2,1,0:T(8,128)(2,1)} %bitcast.108), calls=%async_computation.1 | async-start | bytes 12582912 | tf_op jit(solution)/shard_map/all_to_all | solution.py:124
  353.6 158.4 %reduce-scatter.2.cloned.1.call-start = ((), (), s32[]{:S(2)}) async-start(), calls=%async_computation.6 | async-start | bytes 2228224 | tf_op jit(solution)/shard_map/reduce_scatter | solution.py:129
Sparse Core Ops, SparseCore 0:
  9.8 65.2 all-gather.4
  76.8 39.4 all-gather.2
  118.7 113.3 all-reduce.1
  447.2 64.7 reduce-scatter.1
where the time goes:
time: 521 us; the launch traced here: 520 us
  waiting for transfers between devices  356 us (68%)
  blocking collectives  79 us (15%)
  matrix products  30.6 us (6%)
  local copies, waits for them, and re-layouts  20.5 us (4%)
  other arithmetic  14.3 us (3%)
  between operations  14 us (3%)
  starting transfers between devices  6.07 us (1%)
    psum x1, waiting for transfers between devices, shards(): lax.psum(head_part.astype(jnp.bfloat16), 'tensor').astype(jnp.float32)  116 us
    all_to_all x1, waiting for transfers between devices, shards(): lax.all_to_all(computed, 'expert', split_axis=0, concat_axis=0, tiled=True)  87.2 us
    all_to_all x1, blocking collectives, shards(): lax.all_to_all(outgoing, 'expert', split_axis=0, concat_axis=0, tiled=True)  79 us
    reduce_scatter x1, waiting for transfers between devices, shards(): lax.psum_scatter(expert_part.astype(jnp.bfloat16), 'tensor', scatter_dime...  65 us
    all_gather x1, waiting for transfers between devices, shards(): lax.all_gather(out_proj, 'expert', axis=1, tiled=True)  51.8 us
    all_gather x1, waiting for transfers between devices, shards(): residual_full = lax.all_gather(residual, 'tensor', axis=0, tiled=True)  34.7 us
    gather x1, local copies, waits for them, and re-layouts, shards(): jnp.take(normed_full, source_rows, axis=0)  13.8 us
  transfers between devices with their start and end apart: 5, of which 5 were waited for; matrix products, arithmetic and copies ran while one was open for 4% of the time, Pallas kernels for 0%

commit v1 on v0

--- a/solution.py
+++ b/solution.py
@@ -11,6 +11,17 @@
 HSPLIT = 4
 TOK_DEV = 16
 PREFIX = 1024
+
+
+def record_read(incoming_x):
+    pages = []
+    for _ in range(lax.axis_size("expert")):
+        pages.append(incoming_x)
+    piece_out = lax.all_to_all(
+        jnp.stack(pages, axis=0), axis_name="expert", split_axis=0, concat_axis=0
+    )
+    current_arr = jnp.concatenate(piece_out, 1)
+    return current_arr
 
 
 def norm_rows(hidden_state, norm_gain):
@@ -82,11 +93,7 @@
         .astype(jnp.bfloat16)
         .reshape(step_rows, per_device * HD)
     )
-    head_part = jnp.dot(
-        attended,
-        lax.all_gather(out_proj, "expert", axis=1, tiled=True),
-        preferred_element_type=jnp.float32,
-    )
+    head_part = jnp.dot(attended, record_read(out_proj), preferred_element_type=jnp.float32)
     slot_count = tensor_count // HSPLIT
     experts = expert_count * slot_count
     most_rows = min(TOK_DEV, max(2, TOK_DEV * TOPK // experts + 1))

time: 521 us -> 490 us (0.940)
  waiting for transfers between devices: 356 us -> 314 us
  starting transfers between devices: 6.07 us -> 13.7 us
    all_gather x1 -> x0, waiting for transfers between devices: 51.8 us -> none  [shards(): lax.all_gather(out_proj, 'expert', axis=1, tiled=True)]
    all_to_all x0 -> x1, waiting for transfers between devices: none -> 43.7 us  [record_read(): lax.all_to_all(jnp.stack(pages, axis=0), axis_name='expert', split_axis=0...]
    all_gather x1, waiting for transfers between devices: 34.7 us -> 0.02 us  [shards(): residual_full = lax.all_gather(residual, 'tensor', axis=0, tiled=True)]
    all_to_all x0 -> x1, starting transfers between devices: none -> 7.61 us  [record_read(): lax.all_to_all(jnp.stack(pages, axis=0), axis_name='expert', split_axis=0...]
  transfers between devices with their start and end apart: 5 -> 5, of which waited for: 5 -> 4; matrix products, arithmetic and copies ran while one was open for 4% -> 4% of each run, Pallas kernels for 0% -> 0%
where the time goes in v1:
time: 490 us; the launch traced here: 489 us
  waiting for transfers between devices  314 us (64%)
  blocking collectives  79 us (16%)
  matrix products  30.7 us (6%)
  local copies, waits for them, and re-layouts  24.1 us (5%)
  between operations  14 us (3%)
  starting transfers between devices  13.7 us (3%)
  other arithmetic  13.6 us (3%)
    psum x1, waiting for transfers between devices, shards(): lax.psum(head_part.astype(jnp.bfloat16), 'tensor').astype(jnp.float32)  118 us
    all_to_all x1, waiting for transfers between devices, shards(): lax.all_to_all(computed, 'expert', split_axis=0, concat_axis=0, tiled=True)  87.2 us
    all_to_all x1, blocking collectives, shards(): lax.all_to_all(outgoing, 'expert', split_axis=0, concat_axis=0, tiled=True)  79 us
    reduce_scatter x1, waiting for transfers between devices, shards(): lax.psum_scatter(expert_part.astype(jnp.bfloat16), 'tensor', scatter_dime...  64.9 us
    all_to_all x1, waiting for transfers between devices, record_read(): lax.all_to_all(jnp.stack(pages, axis=0), axis_name='expert', split_axis=0...  43.7 us
    gather x1, local copies, waits for them, and re-layouts, shards(): jnp.take(normed_full, source_rows, axis=0)  13.8 us
  transfers between devices with their start and end apart: 5, of which 4 were waited for; matrix products, arithmetic and copies ran while one was open for 4% of the time, Pallas kernels for 0%

profile of v1, /device:TPU:2, one launch (start us, length us, event | category | flops | bytes accessed | tf_op | source)
XLA Modules:
  0.0 489.2 jit_solution(16437509157023381475)
XLA Ops:
  6.5 0.0 copy-start
  6.5 1.2 copy.38
  7.8 2.4 stack.2
  10.2 7.6 %all-to-all-start = ((bf16[16,512,256]{1,2,0:T(8,128)(2,1)}), bf16[16,512,256]{1,2,0:T(8,128)(2,1)}, u32[]{:S(2)}, u32[]{:S(2)}) async-start(bf16[16,512,256]{1,2,0:T(8,128)(2,1)} %stack.2), calls=%async_computation | async-start | bytes 8388608 | tf_op jit(solution)/shard_map/all_to_all | solution.py:20
  17.8 0.0 all-gather.2.cloned.1.call-start
  17.8 0.7 all-gather.2.cloned.1.call-update
  18.5 0.0 all-reduce.2.cloned.1.call-start
  18.6 0.0 copy-done.2
  18.6 0.1 convert_reduce_fusion
  18.7 0.1 copy.39
  19.5 1.1 copy.41
  20.6 1.9 reduce_window_sum.14
  22.5 2.0 dynamic-slice_bitcast_fusion
  24.6 1.0 fusion.26
  25.6 5.2 %fusion.62 = (f32[4,256]{1,0:T(4,128)S(1)}, bf16[4,256,1280]{1,2,0:T(8,128)(2,1)}) fusion(pred[256,1280]{0,1:T(8,128)(4,1)S(1)} %fusion.26, bf16[1280,256]{1,0:T(8,128)(2,1)} %dynamic-slice_bitcast_fusion, bf16[256,512]{1,0:T(8,128)(2,1)} %param.11), kind=kOutput, calls=%fused_computation.84 | convolution fusion | flops 680264960 | bytes 4460544 | tf_op jit(solution)/shard_map/sub | solution.py:86
  30.8 2.4 fusion.33
  33.2 43.7 %all-to-all-done = bf16[16,512,256]{1,2,0:T(8,128)(2,1)} async-done(((bf16[16,512,256]{1,2,0:T(8,128)(2,1)}), bf16[16,512,256]{1,2,0:T(8,128)(2,1)}, u32[]{:S(2)}, u32[]{:S(2)}) %all-to-all-start) | async-done | bytes 4194336 | tf_op jit(solution)/shard_map/all_to_all | solution.py:20
  76.8 4.8 convolution_convert_fusion.1
  81.7 0.0 all-reduce.2.cloned.1.call-update
  81.7 0.9 fusion.57
  82.6 0.4 select_reduce_fusion
  83.0 0.1 reshape.165
  83.1 0.4 fusion.37
  83.5 0.0 all-gather.2.cloned.1.call-done
  83.5 117.6 %all-reduce.2.cloned.1.call-done = bf16[256,4096]{1,0:T(8,128)(2,1)} async-done(((bf16[256,4096]{1,0:T(8,128)(2,1)}), bf16[256,4096]{1,0:T(8,128)(2,1)}) %all-reduce.2.cloned.1.call-update) | async-done | bytes 2097168 | tf_op jit(solution)/shard_map/psum | solution.py:112
  201.1 3.2 fusion.6
  204.3 0.0 copy-start.1
  204.3 1.3 copy-done.1
  205.7 0.0 copy-done.3
  205.7 2.0 fusion.8
  207.7 13.8 %gather_fusion = bf16[768,4096]{1,0:T(8,128)(2,1)} fusion(bf16[256,4096]{1,0:T(8,128)(2,1)} %fusion.8, s32[1024]{0:T(1024)S(1)} %pad_clamp_fusion), kind=kCustom, calls=%fused_computation | custom fusion | bytes 12585984 | tf_op jit(solution)/shard_map/jit(_take)/gather | solution.py:122
  221.5 3.9 select_select_fusion
  225.4 0.0 copy-start.5
  225.4 79.0 %all_to_all.15 = bf16[16,48,4096]{2,1,0:T(8,128)(2,1)S(1)} all-to-all(bf16[16,48,4096]{2,1,0:T(8,128)(2,1)S(1)} %select_select_fusion), channel_id=1, replica_groups=mesh['expert'=16,'tensor'=16] {'expert'}, dimensions={0} | all-to-all | bytes 12582912 | tf_op jit(solution)/shard_map/all_to_all | solution.py:124
  304.4 0.0 copy-done.5
  304.4 3.4 fusion.12
  307.8 0.0 copy-done.6
  307.8 3.5 fusion.22
  311.3 0.0 copy-done
  311.3 5.4 %convolution_convert_fusion = bf16[768,4096]{1,0:T(8,128)(2,1)} fusion(bf16[768,384]{1,0:T(8,128)(2,1)S(1)} %fusion.22, bf16[1,384,4096]{2,1,0:T(8,128)(2,1)S(1)} %copy-done), kind=kOutput, calls=%fused_computation.2 | convolution fusion | flops 2419064832 | bytes 10027008 | tf_op jit(solution)/shard_map/dot_general | solution.py:129
  316.7 6.0 %all-to-all-start.2 = ((bf16[16,48,4096]{2,1,0:T(8,128)(2,1)}), bf16[16,48,4096]{2,1,0:T(8,128)(2,1)}, u32[]{:S(2)}, u32[]{:S(2)}) async-start(bf16[16,48,4096]{2,1,0:T(8,128)(2,1)} %bitcast.111), calls=%async_computation.2 | async-start | bytes 12582912 | tf_op jit(solution)/shard_map/all_to_all | solution.py:131
  322.7 0.0 reduce-scatter.2.cloned.1.call-start
  322.7 0.1 select_reduce_fusion.1
  322.9 87.2 %all-to-all-done.2 = bf16[16,48,4096]{2,1,0:T(8,128)(2,1)} async-done(((bf16[16,48,4096]{2,1,0:T(8,128)(2,1)}), bf16[16,48,4096]{2,1,0:T(8,128)(2,1)}, u32[]{:S(2)}, u32[]{:S(2)}) %all-to-all-start.2) | async-done | bytes 6291488 | tf_op jit(solution)/shard_map/all_to_all | solution.py:131
  410.1 6.0 %fusion.3 = bf16[256,4096]{1,0:T(8,128)(2,1)} fusion(bf16[16,48,4096]{2,1,0:T(8,128)(2,1)} %all-to-all-done.2, bf16[256,16]{0,1:T(8,128)(2,1)S(1)} %bitcast.122, s32[256,16]{0,1:T(8,128)S(1)} %bitcast.116, pred[256,16]{0,1:T(8,128)(4,1)S(1)} %bitcast.121), kind=kOutput, calls=%fused_computation.11 | convolution fusion | flops 1612251136 | bytes 8417280 | tf_op jit(solution)/shard_map/njc,jcd->nd/dot_general | solution.py:133
  416.1 0.0 reduce-scatter.2.cloned.1.call-update
  416.1 64.9 %reduce-scatter.2.cloned.1.call-done = bf16[16,4096]{1,0:T(8,128)(2,1)} async-done(((bf16[256,4096]{1,0:T(8,128)(2,1)}), bf16[16,4096]{1,0:T(8,128)(2,1)}) %reduce-scatter.2.cloned.1.call-update) | async-done | bytes 131088 | tf_op jit(solution)/shard_map/reduce_scatter | solution.py:136
  481.0 1.7 add_convert_fusion.1
  (21 shorter events, 0.2 us)
Async XLA Ops:
  6.5 304.7 %copy-start = (bf16[1,384,4096]{2,1,0:T(8,128)(2,1)S(1)}, bf16[1,384,4096]{2,1,0:T(8,128)(2,1)}, u32[]{:S(2)}) copy-start(bf16[1,384,4096]{2,1,0:T(8,128)(2,1)} %param.21) | copy-start | bytes 9437188
  10.2 8.4 %copy-start.2 = (s32[256,8]{0,1:T(8,128)S(1)}, s32[256,8]{0,1:T(8,128)}, u32[]{:S(2)}) copy-start(s32[256,8]{0,1:T(8,128)} %param.17) | copy-start | bytes 24580
  10.2 66.7 %all-to-all-start = ((bf16[16,512,256]{1,2,0:T(8,128)(2,1)}), bf16[16,512,256]{1,2,0:T(8,128)(2,1)}, u32[]{:S(2)}, u32[]{:S(2)}) async-start(bf16[16,512,256]{1,2,0:T(8,128)(2,1)} %stack.2), calls=%async_computation | async-start | bytes 8388608 | tf_op jit(solution)/shard_map/all_to_all | solution.py:20
  17.8 65.7 %all-gather.2.cloned.1.call-start = ((), (), s32[]{:S(2)}) async-start(), calls=%async_computation.4 | async-start | bytes 2228224 | tf_op jit(solution)/shard_map/all_gather | solution.py:113
  18.5 182.6 %all-reduce.2.cloned.1.call-start = ((), (), s32[]{:S(2)}) async-start(), calls=%async_computation.5 | async-start | bytes 4194304 | tf_op jit(solution)/shard_map/psum | solution.py:112
  81.7 124.0 %copy-start.3 = (f32[4096]{0:T(1024)S(1)}, f32[4096]{0:T(1024)}, u32[]{:S(2)}) copy-start(f32[4096]{0:T(1024)} %param.16) | copy-start | bytes 49156
  204.3 1.4 copy-start.1
  225.4 79.0 %copy-start.5 = (bf16[1,4096,384]{2,1,0:T(8,128)(2,1)S(1)}, bf16[1,4096,384]{2,1,0:T(8,128)(2,1)}, u32[]{:S(2)}) copy-start(bf16[1,4096,384]{2,1,0:T(8,128)(2,1)} %param.19) | copy-start | bytes 9437188
  304.4 3.4 copy-start.6
  316.7 6.0 %copy-start.4 = (bf16[256,8]{0,1:T(8,128)(2,1)S(1)}, bf16[256,8]{0,1:T(8,128)(2,1)}, u32[]{:S(2)}) copy-start(bf16[256,8]{0,1:T(8,128)(2,1)} %param.18) | copy-start | bytes 12292
  316.7 93.4 %all-to-all-start.2 = ((bf16[16,48,4096]{2,1,0:T(8,128)(2,1)}), bf16[16,48,4096]{2,1,0:T(8,128)(2,1)}, u32[]{:S(2)}, u32[]{:S(2)}) async-start(bf16[16,48,4096]{2,1,0:T(8,128)(2,1)} %bitcast.111), calls=%async_computation.2 | async-start | bytes 12582912 | tf_op jit(solution)/shard_map/all_to_all | solution.py:131
  322.7 158.4 %reduce-scatter.2.cloned.1.call-start = ((), (), s32[]{:S(2)}) async-start(), calls=%async_computation.6 | async-start | bytes 2228224 | tf_op jit(solution)/shard_map/reduce_scatter | solution.py:136
Sparse Core Ops, SparseCore 0:
  20.4 42.4 all-gather.1
  81.8 119.2 all-reduce.1
  416.2 64.7 reduce-scatter.1
